TPU v7x, 256 devices: a whole 4x4x8 slice. The times are simulated.
256 devices in a mesh: seq: 32 (over y, x, core), head: 8 (over z).
Axes of the slice: x: 4, y: 4, z: 8, core: 2. Of those that a mesh axis runs over, the one named last changes fastest.
Arguments:
- tokens: bfloat16 [32768, 2048], P(('seq', 'head')), may hold values from -6 to 6
- w_qkv: bfloat16 [2048, 3, 2048], P(None, None, 'head'), may hold values from -0.125 to 0.125
- w_beta: bfloat16 [2048, 16], P(None, 'head'), may hold values from -0.125 to 0.125
- beta_bias: float32 [16], P('head'), may hold values from -8 to 2
- w_out: bfloat16 [2048, 2048], P('head'), may hold values from -0.125 to 0.125
Outputs:
- mixed: bfloat16 [32768, 2048], P(('seq', 'head'))
All inputs are finite; a program needn't handle non-finite values.
Results may differ from a plain program's by a relative error of at most 0.015.
Values may be sent and summed in bfloat16 or wider, within the bound.
A program may use at most 64 MiB of HBM per device.

v0:
```python
import jax
import jax.numpy as jnp
from jax import lax
from jax.sharding import PartitionSpec as P

C = 64
epsilon = 1e-06


def unit_norm(values):
    return values * lax.rsqrt(jnp.sum(values * values, -1, keepdims=True) + epsilon)


def prepare(queries, key_rows, value_rows, strength):
    highest = lax.Precision.HIGHEST
    size_k = key_rows.shape[-1]
    similar = jnp.einsum("...id,...jd->...ij", key_rows, key_rows, precision=highest)
    system = jnp.eye(C, dtype=jnp.float32) + jnp.tril(similar * strength[..., :, None], -1)
    weighted = jnp.concatenate(
        [strength[..., None] * key_rows, strength[..., None] * value_rows], -1
    )
    solved = jax.scipy.linalg.solve_triangular(system, weighted, lower=True, unit_diagonal=True)
    w_fac = solved[..., :size_k]
    u_fac = solved[..., size_k:]
    masked = jnp.tril(jnp.einsum("...id,...jd->...ij", queries, key_rows, precision=highest))
    q_eff = queries - jnp.einsum("...ij,...jd->...id", masked, w_fac, precision=highest)
    return (w_fac, u_fac, masked, q_eff)


def body(tokens, w_qkv, w_beta, beta_bias, w_out):
    highest = lax.Precision.HIGHEST
    float_tokens = tokens.astype(jnp.float32)
    normed = (
        float_tokens * lax.rsqrt(jnp.mean(float_tokens * float_tokens, -1, keepdims=True) + epsilon)
    ).astype(jnp.bfloat16)
    gathered = lax.all_gather(normed, "head", axis=0, tiled=True)
    length = gathered.shape[0]
    model_width = gathered.shape[1]
    local_heads = beta_bias.shape[0]
    size_k = w_out.shape[0] // local_heads
    projected = jnp.dot(
        gathered, w_qkv.reshape(model_width, -1), preferred_element_type=jnp.float32
    )
    projected = projected.reshape(length, 3, local_heads, size_k)
    queries = unit_norm(jax.nn.silu(projected[:, 0]))
    key_rows = unit_norm(jax.nn.silu(projected[:, 1]))
    value_rows = jax.nn.silu(projected[:, 2])
    strength = jax.nn.sigmoid(
        jnp.dot(gathered, w_beta, preferred_element_type=jnp.float32) + beta_bias
    )
    block_count = length // C

    def blocks(values):
        return values.reshape(block_count, C, local_heads, -1).transpose(0, 2, 1, 3)

    key_blocks = blocks(key_rows)
    w_fac, u_fac, masked, q_eff = prepare(
        blocks(queries),
        key_blocks,
        blocks(value_rows),
        strength.reshape(block_count, C, local_heads).transpose(0, 2, 1),
    )
    identity = jnp.broadcast_to(jnp.eye(size_k, dtype=jnp.float32), (local_heads, size_k, size_k))
    empty_state = jnp.zeros((local_heads, size_k, size_k), jnp.float32)

    def advance(pair_state, pieces):
        transition, state = pair_state
        w_blk, u_blk, m_blk, qe_blk, k_blk = pieces
        local_out = jnp.einsum("hcj,hvj->hcv", qe_blk, state, precision=highest) + jnp.einsum(
            "hcd,hdv->hcv", m_blk, u_blk, precision=highest
        )
        fold_query = jnp.einsum("hcj,hij->hci", qe_blk, transition, precision=highest)
        trans_w = jnp.einsum("hij,hcj->hic", transition, w_blk, precision=highest)
        new_transition = transition - jnp.einsum("hic,hcd->hid", trans_w, k_blk, precision=highest)
        state_w = jnp.einsum("hvj,hcj->hvc", state, w_blk, precision=highest)
        change = u_blk.transpose(0, 2, 1) - state_w
        new_state = state + jnp.einsum("hvc,hcd->hvd", change, k_blk, precision=highest)
        return ((new_transition, new_state), (local_out, fold_query))

    (trans_end, state_end), (local_all, fold_all) = lax.scan(
        advance, (identity, empty_state), (w_fac, u_fac, masked, q_eff, key_blocks)
    )
    all_trans, all_state = (
        lax.all_gather(trans_end[None].astype(jnp.bfloat16), "seq", axis=0, tiled=True).astype(
            jnp.float32
        ),
        lax.all_gather(state_end[None].astype(jnp.bfloat16), "seq", axis=0, tiled=True).astype(
            jnp.float32
        ),
    )
    own_index = lax.axis_index("seq")

    def chain_step(state, pieces):
        transition, partial_value, position = pieces
        advanced = jnp.einsum("hvj,hjk->hvk", state, transition, precision=highest) + partial_value
        return (jnp.where(position < own_index, advanced, state), None)

    incoming, _ = lax.scan(
        chain_step,
        empty_state,
        (all_trans, all_state, jnp.arange(all_trans.shape[0], dtype=jnp.int32)),
    )
    outputs = local_all + jnp.einsum("nhci,hvi->nhcv", fold_all, incoming, precision=highest)
    outputs = outputs.transpose(0, 2, 1, 3).reshape(length, local_heads, size_k)
    outputs = outputs * lax.rsqrt(jnp.mean(outputs * outputs, -1, keepdims=True) + epsilon)
    flat_out = outputs.reshape(length, local_heads * size_k).astype(jnp.bfloat16)
    return lax.psum_scatter(
        jnp.dot(flat_out, w_out, preferred_element_type=jnp.float32).astype(jnp.bfloat16),
        "head",
        scatter_dimension=0,
        tiled=True,
    )


def solution(mesh):
    return jax.shard_map(
        body,
        mesh=mesh,
        in_specs=(
            P(("seq", "head"), None),
            P(None, None, "head"),
            P(None, "head"),
            P("head"),
            P("head", None),
        ),
        out_specs=P(("seq", "head"), None),
        check_vma=False,
    )
```

profile of v0, /device:TPU:1, one launch (start us, length us, event | category | flops | bytes accessed | tf_op | source)
XLA Modules:
  0.0 669.9 jit_solution(6696784962300135828)
XLA Ops:
  7.9 2.0 fusion.63
  10.0 4.8 copy.39
  14.8 53.6 %all-gather.6.cloned.1.call-done = bf16[1024,2048]{1,0:T(8,128)(2,1)} async-done(((bf16[128,2048]{1,0:T(8,128)(2,1)}), bf16[1024,2048]{1,0:T(8,128)(2,1)}) %all-gather.6.cloned.1.call-update) | async-done | bytes 4194320 | tf_op jit(solution)/shard_map/all_gather | solution.py:36
  68.4 6.2 fusion.45
  77.2 3.4 fusion.61
  80.7 2.7 broadcast_multiply_fusion
  83.4 2.7 fusion.57
  86.1 158.7 %custom-call.4 = f32[16,2,1,64,64]{3,4,2,1,0:T(8,128)} custom-call(f32[16,2,1,64,64]{4,3,2,1,0:T(8,128)} %fusion.57), custom_call_target="InvertDiagBlocksLowerTriangular" | custom-call | tf_op jit(solution)/shard_map/jit(_solve_triangular)/vmap(vmap())/triangular_solve | solution.py:22
  244.9 3.5 fusion.47
  249.7 2.0 convolution_select_fusion
  251.7 2.4 convolution_subtract_fusion.2
  254.2 127.7 %while.28 = (s32[]{:T(128)}, f32[2,128,128]{2,1,0:T(8,128)S(1)}, f32[2,128,128]{2,1,0:T(8,128)S(1)}, f32[16,2,64,128]{3,2,0,1:T(8,128)}, f32[16,2,64,128]{3,2,0,...) while((s32[]{:T(128)}, f32[2,128,128]{2,1,0:T(8,128)S(1)}, ...), condition=%wide.region_4.5_spmd.clone, body=%wide.region_3.4_spmd.clone.sunk | while | flops 163774464 | bytes 2167433 | solution.py:80
  258.8 1.8 fusion.138
  266.8 1.8 fusion.138
  322.6 1.8 fusion.138
  346.5 1.8 fusion.138
  383.3 47.1 %all-gather.8.cloned.1.call-done = bf16[64,128,128]{2,1,0:T(8,128)(2,1)} async-done(((bf16[2,128,128]{2,1,0:T(8,128)(2,1)}), bf16[64,128,128]{2,1,0:T(8,128)(2,1)}) %all-gather.8.cloned.1.call-update) | async-done | bytes 2097168 | tf_op jit(solution)/shard_map/all_gather | solution.py:84
  430.4 4.1 convert.3
  434.5 46.5 %all-gather.10.cloned.1.call-done = bf16[64,128,128]{2,1,0:T(8,128)(2,1)} async-done(((bf16[2,128,128]{2,1,0:T(8,128)(2,1)}), bf16[64,128,128]{2,1,0:T(8,128)(2,1)}) %all-gather.10.cloned.1.call-update) | async-done | bytes 2097168 | tf_op jit(solution)/shard_map/all_gather | solution.py:87
  481.0 4.1 convert.4
  485.1 115.8 %while.29 = (s32[]{:T(128)}, f32[2,128,128]{1,2,0:T(8,128)S(1)}, s32[32]{0:T(128)S(1)}, s32[]{:T(128)}, f32[32,2,128,128]{3,2,1,0:T(8,128)}, /*index=5*/f32[32,2,128,128]{3,2,1,0:T(8,128)}, s32[]{:T(128)}, s32[]{:T(128)}) while((s32[]{:T(128)}, f32[2,128,128]{1,2,0:T(8,128)S(1)}, s32[32]{0:T(128)S(1)}, s32[]{:T(128)}, ...), condition=%wide.region_6.7_spmd.clone, body=%wide.region_5.6_spmd.clone.sunk | while | flops 50462724 | bytes 1443959 | solution.py:98
  600.9 2.4 multiply_reduce_fusion
  605.6 3.2 convolution_convert_fusion
  608.9 54.4 %reduce-scatter.2.cloned.1.call-done = bf16[128,2048]{1,0:T(8,128)(2,1)} async-done(((bf16[1024,2048]{1,0:T(8,128)(2,1)}), bf16[128,2048]{1,0:T(8,128)(2,1)}) %reduce-scatter.2.cloned.1.call-update) | async-done | bytes 524304 | tf_op jit(solution)/shard_map/reduce_scatter | solution.py:107
  (317 shorter events, 221.8 us)
Async XLA Ops:
  6.5 599.1 %copy-start = (bf16[256,2048]{1,0:T(8,128)(2,1)S(1)}, bf16[256,2048]{1,0:T(8,128)(2,1)}, u32[]{:S(2)}) copy-start(bf16[256,2048]{1,0:T(8,128)(2,1)} %param.13) | copy-start | bytes 3145732
  6.5 61.9 %all-gather.6.cloned.1.call-start = ((), (), s32[]{:S(2)}) async-start(), calls=%async_computation.1 | async-start | bytes 4718592 | tf_op jit(solution)/shard_map/all_gather | solution.py:36
  9.9 420.6 %all-gather.8.cloned.1.call-start = ((), (), s32[]{:S(2)}) async-start(), calls=%async_computation.3 | async-start | bytes 2162688 | tf_op jit(solution)/shard_map/all_gather | solution.py:84
  75.3 1.8 copy-start.4
  75.3 1.8 copy-start.5
  248.4 1.3 copy-start.2
  251.7 2.5 copy-start.3
  382.5 98.5 %all-gather.10.cloned.1.call-start = ((), (), s32[]{:S(2)}) async-start(), calls=%async_computation.4 | async-start | bytes 2162688 | tf_op jit(solution)/shard_map/all_gather | solution.py:87
  383.3 280.0 %reduce-scatter.2.cloned.1.call-start = ((), (), s32[]{:S(2)}) async-start(), calls=%async_computation.2 | async-start | bytes 4718592 | tf_op jit(solution)/shard_map/reduce_scatter | solution.py:107
  485.1 115.8 %copy-start.1 = (f32[16,2,64,128]{3,2,0,1:T(8,128)S(1)}, f32[16,2,64,128]{3,2,0,1:T(8,128)}, u32[]{:S(2)}) copy-start(f32[16,2,64,128]{3,2,0,1:T(8,128)} %get-tuple-element.92) | copy-start | bytes 3145732
Sparse Core Ops, SparseCore 0:
  10.0 58.3 all-gather.5
  382.7 47.7 all-gather.7
  433.0 47.9 all-gather.9
  609.0 54.2 reduce-scatter.1
where the time goes:
time: 675 us; the launch traced here: 670 us
  waiting for transfers between devices  202 us (30%)
  matrix products  194 us (29%)
  other arithmetic  175 us (26%)
  local copies, waits for them, and re-layouts  61.9 us (9%)
  loops' own time  23.5 us (3%)
  between operations  13.4 us (2%)
    another operation x4, other arithmetic, prepare(): jax.scipy.linalg.solve_triangular(system, weighted, lower=True, unit_diag...  159 us
    reduce_scatter x1, waiting for transfers between devices, body(): lax.psum_scatter(jnp.dot(flat_out, w_out, preferred_element_type=jnp.floa...  54.4 us
    all_gather x1, waiting for transfers between devices, body(): gathered = lax.all_gather(normed, 'head', axis=0, tiled=True)  53.6 us
    dynamic_slice x96, local copies, waits for them, and re-layouts, body(): lax.scan(chain_step, empty_state, (all_trans, all_state, jnp.arange(all_t...  51.2 us
    all_gather x1, waiting for transfers between devices, body(): lax.all_gather(trans_end[None].astype(jnp.bfloat16), 'seq', axis=0, tiled...  47.1 us
    all_gather x1, waiting for transfers between devices, body(): lax.all_gather(state_end[None].astype(jnp.bfloat16), 'seq', axis=0, tiled...  46.5 us
    dot_general x32, matrix products, chain_step(): jnp.einsum('hvj,hjk->hvk', state, transition, precision=highest)  41.8 us
    dot_general x16, matrix products, advance(): jnp.einsum('hcj,hij->hci', qe_blk, transition, precision=highest)  29.4 us
  transfers between devices with their start and end apart: 4, of which 4 were waited for; matrix products, arithmetic and copies ran while one was open for 1% of the time, Pallas kernels for 0%

commit v1 on v0

--- a/solution.py
+++ b/solution.py
@@ -84,9 +84,15 @@
         lax.all_gather(trans_end[None].astype(jnp.bfloat16), "seq", axis=0, tiled=True).astype(
             jnp.float32
         ),
-        lax.all_gather(state_end[None].astype(jnp.bfloat16), "seq", axis=0, tiled=True).astype(
-            jnp.float32
-        ),
+        jnp.concatenate(
+            lax.all_to_all(
+                jnp.stack([state_end[None].astype(jnp.bfloat16)] * lax.axis_size("seq")),
+                "seq",
+                0,
+                0,
+            ),
+            axis=0,
+        ).astype(jnp.float32),
     )
     own_index = lax.axis_index("seq")
 

time: 675 us -> 606 us (0.90)
  waiting for transfers between devices: 202 us -> 157 us
  local copies, waits for them, and re-layouts: 61.9 us -> 31.4 us
  starting transfers between devices: 0.13 us -> 7.78 us
    all_gather x1 -> x0, waiting for transfers between devices: 46.5 us -> none  [body(): lax.all_gather(state_end[None].astype(jnp.bfloat16), 'seq', axis=0, tiled...]
    dynamic_slice x96 -> x32, local copies, waits for them, and re-layouts: 51.2 us -> 18.8 us  [body(): lax.scan(chain_step, empty_state, (all_trans, all_state, jnp.arange(all_t...]
    all_to_all x0 -> x1, waiting for transfers between devices: none -> 29.7 us  [body(): lax.all_to_all(jnp.stack([state_end[None].astype(jnp.bfloat16)] * lax.axi...]
    all_gather x1, waiting for transfers between devices: 47.1 us -> 18.8 us  [body(): lax.all_gather(trans_end[None].astype(jnp.bfloat16), 'seq', axis=0, tiled...]
    all_to_all x0 -> x1, starting transfers between devices: none -> 7.7 us  [body(): lax.all_to_all(jnp.stack([state_end[None].astype(jnp.bfloat16)] * lax.axi...]
  transfers between devices with their start and end apart: 4 -> 4, of which waited for: 4 -> 4; matrix products, arithmetic and copies ran while one was open for 1% -> 2% of each run, Pallas kernels for 0% -> 0%
where the time goes in v1:
time: 606 us; the launch traced here: 601 us
  matrix products  196 us (32%)
  other arithmetic  173 us (29%)
  waiting for transfers between devices  157 us (26%)
  local copies, waits for them, and re-layouts  31.4 us (5%)
  loops' own time  23.1 us (4%)
  between operations  13.4 us (2%)
  starting transfers between devices  7.78 us (1%)
    another operation x4, other arithmetic, prepare(): jax.scipy.linalg.solve_triangular(system, weighted, lower=True, unit_diag...  159 us
    reduce_scatter x1, waiting for transfers between devices, body(): lax.psum_scatter(jnp.dot(flat_out, w_out, preferred_element_type=jnp.floa...  54.4 us
    all_gather x1, waiting for transfers between devices, body(): gathered = lax.all_gather(normed, 'head', axis=0, tiled=True)  53.6 us
    dot_general x32, matrix products, chain_step(): jnp.einsum('hvj,hjk->hvk', state, transition, precision=highest)  43.9 us
    all_to_all x1, waiting for transfers between devices, body(): lax.all_to_all(jnp.stack([state_end[None].astype(jnp.bfloat16)] * lax.axi...  29.7 us
    dot_general x16, matrix products, advance(): jnp.einsum('hcj,hij->hci', qe_blk, transition, precision=highest)  29.2 us
    dot_general x16, matrix products, advance(): jnp.einsum('hcd,hdv->hcv', m_blk, u_blk, precision=highest)  26.6 us
    another operation x1, loops' own time, body(): lax.scan(chain_step, empty_state, (all_trans, all_state, jnp.arange(all_t...  22.1 us
  transfers between devices with their start and end apart: 4, of which 4 were waited for; matrix products, arithmetic and copies ran while one was open for 2% of the time, Pallas kernels for 0%

profile of v1, /device:TPU:1, one launch (start us, length us, event | category | flops | bytes accessed | tf_op | source)
XLA Modules:
  0.0 601.1 jit_solution(12823991996359406437)
XLA Ops:
  7.9 2.0 fusion.63
  10.0 4.7 copy.39
  14.8 53.6 %all-gather.4.cloned.1.call-done = bf16[1024,2048]{1,0:T(8,128)(2,1)} async-done(((bf16[128,2048]{1,0:T(8,128)(2,1)}), bf16[1024,2048]{1,0:T(8,128)(2,1)}) %all-gather.4.cloned.1.call-update) | async-done | bytes 4194320 | tf_op jit(solution)/shard_map/all_gather | solution.py:36
  68.4 6.2 %fusion.45 = f32[1024,3,2,128]{3,0,2,1:T(8,128)S(1)} fusion(bf16[3,2,128,2048]{3,2,1,0:T(8,128)(2,1)} %bitcast.200, bf16[1024,2048]{1,0:T(8,128)(2,1)} %all-gather.4.cloned.1.call-done), kind=kOutput, calls=%fused_computation.51 | convolution fusion | flops 3221225472 | bytes 10485760 | tf_op jit(solution)/shard_map/dot_general | solution.py:41
  77.2 3.4 fusion.61
  80.7 2.7 broadcast_multiply_fusion
  83.4 2.8 fusion.57
  86.1 158.7 %custom-call.4 = f32[16,2,1,64,64]{3,4,2,1,0:T(8,128)} custom-call(f32[16,2,1,64,64]{4,3,2,1,0:T(8,128)} %fusion.57), custom_call_target="InvertDiagBlocksLowerTriangular" | custom-call | tf_op jit(solution)/shard_map/jit(_solve_triangular)/vmap(vmap())/triangular_solve | solution.py:22
  244.9 3.5 fusion.47
  249.7 2.0 convolution_select_fusion
  251.7 2.4 convolution_subtract_fusion.2
  254.2 127.3 %while.28 = (s32[]{:T(128)}, f32[2,128,128]{2,1,0:T(8,128)S(1)}, f32[2,128,128]{2,1,0:T(8,128)S(1)}, f32[16,2,64,128]{3,2,0,1:T(8,128)}, f32[16,2,64,128]{3,2,0,...) while((s32[]{:T(128)}, f32[2,128,128]{2,1,0:T(8,128)S(1)}, ...), condition=%wide.region_4.5_spmd.clone, body=%wide.region_3.4_spmd.clone.sunk | while | flops 163774464 | bytes 2167433 | solution.py:80
  322.4 1.8 fusion.138
  330.4 1.8 fusion.138
  382.3 1.8 stack.2
  384.1 7.7 %all-to-all-start = ((bf16[32,1,2,128,128]{3,4,2,1,0:T(8,128)(2,1)}), bf16[32,1,2,128,128]{3,4,2,1,0:T(8,128)(2,1)S(1)}, u32[]{:S(2)}, u32[]{:S(2)}) async-start(bf16[32,1,2,128,128]{3,4,2,1,0:T(8,128)(2,1)} %stack.2), calls=%async_computation | async-start | bytes 4194304 | tf_op jit(solution)/shard_map/all_to_all | solution.py:88
  391.9 29.7 %all-to-all-done = bf16[32,1,2,128,128]{3,4,2,1,0:T(8,128)(2,1)S(1)} async-done(((bf16[32,1,2,128,128]{3,4,2,1,0:T(8,128)(2,1)}), bf16[32,1,2,128,128]{3,4,2,1,0:T(8,128)(2,1)S(1)}, u32[]{:S(2)}, u32[]{:S(2)}) %all-to-all-start) | async-done | bytes 2097184 | tf_op jit(solution)/shard_map/all_to_all | solution.py:88
  421.6 2.5 bitcast_convert_fusion
  424.1 18.8 %all-gather.6.cloned.1.call-done = bf16[64,128,128]{2,1,0:T(8,128)(2,1)} async-done(((bf16[2,128,128]{2,1,0:T(8,128)(2,1)}), bf16[64,128,128]{2,1,0:T(8,128)(2,1)}) %all-gather.6.cloned.1.call-update) | async-done | bytes 2097168 | tf_op jit(solution)/shard_map/all_gather | solution.py:84
  442.9 4.2 convert.4
  447.1 85.0 %while.29 = (s32[]{:T(128)}, f32[2,128,128]{1,2,0:T(8,128)S(1)}, s32[32]{0:T(128)S(1)}, s32[]{:T(128)}, f32[32,2,128,128]{3,2,1,0:T(8,128)}, /*index=5*/f32[32,2,128,128]{2,3,1,0:T(8,128)}, s32[]{:T(128)}, s32[]{:T(128)}) while((s32[]{:T(128)}, f32[2,128,128]{1,2,0:T(8,128)S(1)}, s32[32]{0:T(128)S(1)}, s32[]{:T(128)}, ...), condition=%wide.region_6.7_spmd.clone, body=%wide.region_5.6_spmd.clone.sunk | while | flops 50462724 | bytes 920179 | solution.py:104
  532.1 2.4 multiply_reduce_fusion
  536.9 3.2 convolution_convert_fusion
  540.2 54.4 %reduce-scatter.2.cloned.1.call-done = bf16[128,2048]{1,0:T(8,128)(2,1)} async-done(((bf16[1024,2048]{1,0:T(8,128)(2,1)}), bf16[128,2048]{1,0:T(8,128)(2,1)}) %reduce-scatter.2.cloned.1.call-update) | async-done | bytes 524304 | tf_op jit(solution)/shard_map/reduce_scatter | solution.py:113
  (254 shorter events, 194.2 us)
Async XLA Ops:
  6.5 530.4 %copy-start = (bf16[256,2048]{1,0:T(8,128)(2,1)S(1)}, bf16[256,2048]{1,0:T(8,128)(2,1)}, u32[]{:S(2)}) copy-start(bf16[256,2048]{1,0:T(8,128)(2,1)} %param.13) | copy-start | bytes 3145732
  6.5 61.9 %all-gather.4.cloned.1.call-start = ((), (), s32[]{:S(2)}) async-start(), calls=%async_computation.2 | async-start | bytes 4718592 | tf_op jit(solution)/shard_map/all_gather | solution.py:36
  9.9 433.0 %all-gather.6.cloned.1.call-start = ((), (), s32[]{:S(2)}) async-start(), calls=%async_computation.4 | async-start | bytes 2162688 | tf_op jit(solution)/shard_map/all_gather | solution.py:84
  75.3 1.9 copy-start.4
  75.3 1.9 copy-start.5
  248.4 1.3 copy-start.2
  251.7 2.5 copy-start.3
  384.1 37.4 %all-to-all-start = ((bf16[32,1,2,128,128]{3,4,2,1,0:T(8,128)(2,1)}), bf16[32,1,2,128,128]{3,4,2,1,0:T(8,128)(2,1)S(1)}, u32[]{:S(2)}, u32[]{:S(2)}) async-start(bf16[32,1,2,128,128]{3,4,2,1,0:T(8,128)(2,1)} %stack.2), calls=%async_computation | async-start | bytes 4194304 | tf_op jit(solution)/shard_map/all_to_all | solution.py:88
  391.8 202.7 %reduce-scatter.2.cloned.1.call-start = ((), (), s32[]{:S(2)}) async-start(), calls=%async_computation.3 | async-start | bytes 4718592 | tf_op jit(solution)/shard_map/reduce_scatter | solution.py:113
  442.9 89.2 %copy-start.1 = (f32[16,2,64,128]{3,2,0,1:T(8,128)S(1)}, f32[16,2,64,128]{3,2,0,1:T(8,128)}, u32[]{:S(2)}) copy-start(f32[16,2,64,128]{3,2,0,1:T(8,128)} %get-tuple-element.92) | copy-start | bytes 3145732
Sparse Core Ops, SparseCore 0:
  10.0 58.3 all-gather.3
  382.3 60.6 all-gather.5
  540.3 54.2 reduce-scatter.1
